TPU v7x, 512 devices: a whole 4x8x8 slice. The times are simulated.
512 devices in a mesh: ctx: 64 (over y_hi, z, x), head: 8 (over y_lo, core).
Axes of the slice: x: 4, y: 8 (y_hi: 2, y_lo: 4; y = y_hi * 4 + y_lo), z: 8, core: 2. Of those that a mesh axis runs over, the one named last changes fastest.
Arguments:
- queries: bfloat16 [32768, 1024], P('ctx', 'head'), may hold values from -5 to 5
- keys: bfloat16 [32768, 128], P('ctx'), may hold values from -4 to 4
- values: bfloat16 [32768, 128], P('ctx'), may hold values from -6 to 6
- doc_lengths: int32 [16], replicated, may hold values from 1 to 4096, 32768 in all
- span_order: int32 [128], replicated, may hold values from 0 to 127, as said below
Outputs:
- attended: bfloat16 [32768, 1024], P('ctx', 'head')
Inputs may be any that keep to these rules, and one draw needn't show every extreme that they name: `span_order`: stored spans 2 i and 2 i + 1 (those of ctx index i) are pack spans i and 127-i, in either order. `doc_lengths`: the lengths sum to 32768; the longest is exactly 4096.
All inputs are finite; a program needn't handle non-finite values.
Results may differ from a plain program's by a relative error of at most 0.0044.
Values may be sent and summed in bfloat16 or wider, within the bound.
No kernel may reach another device: no remote copies, remote signals or barrier semaphores. Data moves between devices by JAX's collectives and lax.ppermute only.
A program may use at most 64 MiB of HBM per device.

v0:
```python
import math

import jax
import jax.numpy as jnp
from jax import lax
from jax.sharding import PartitionSpec as P

DH = 128


NEGATIVE = -1e30


def shifted(value, axis, steps):
    count = lax.axis_size(axis)
    leading, last = (max(0, -steps), min(count, count - steps))
    return lax.ppermute(value, axis, [(source, source + steps) for source in range(leading, last)])


def locate(rows, span_order, ends, span_rows):
    span = rows // span_rows
    numbers = jnp.arange(span_order.shape[0], dtype=jnp.int32)
    table = jnp.sum(jnp.where(span[:, None] == numbers[None, :], span_order[None, :], 0), axis=1)
    places = table * span_rows + rows % span_rows
    owners = jnp.sum((places[:, None] >= ends[None, :]).astype(jnp.int32), axis=1)
    return (places, owners)


def absorb(state, query_heads, visible, key_block, value_block):
    running_max, running_sum, numerator = state
    scale = 1.0 / math.sqrt(query_heads.shape[2])
    scores = (
        jnp.einsum("thd,sd->hts", query_heads, key_block, preferred_element_type=jnp.float32)
        * scale
    )
    masked = jnp.where(visible[None], scores, NEGATIVE)
    newmax = jnp.maximum(running_max, jnp.max(masked, axis=2))
    weights = jnp.where(visible[None], jnp.exp(masked - newmax[:, :, None]), 0.0)
    factor = jnp.exp(running_max - newmax)
    running_sum = running_sum * factor + jnp.sum(weights, axis=2)
    numerator = numerator * factor[:, :, None] + jnp.einsum(
        "hts,sd->htd", weights.astype(jnp.bfloat16), value_block, preferred_element_type=jnp.float32
    )
    return (newmax, running_sum, numerator)


def body(queries, keys, values, doc_lengths, span_order):
    local_rows = queries.shape[0]
    head_count = queries.shape[1] // DH
    span_rows = local_rows // 2
    ends = jnp.cumsum(doc_lengths)
    position = lax.axis_index("ctx")
    ctx_count = lax.axis_size("ctx")
    local_range = jnp.arange(local_rows, dtype=jnp.int32)
    query_rows = position * local_rows + local_range
    query_places, query_owners = locate(query_rows, span_order, ends, span_rows)
    query_heads = queries.reshape(local_rows, head_count, DH)
    initial = (
        jnp.full((head_count, local_rows), NEGATIVE, jnp.float32),
        jnp.zeros((head_count, local_rows), jnp.float32),
        jnp.zeros((head_count, local_rows, DH), jnp.float32),
    )

    def consume(state, block_keys, block_values, rows, usable):
        key_places, key_owners = locate(rows, span_order, ends, span_rows)
        visible = (
            usable[None, :]
            & (query_owners[:, None] == key_owners[None, :])
            & (key_places[None, :] <= query_places[:, None])
        )
        return absorb(state, query_heads, visible, block_keys, block_values)

    def remote(state, turn, low_keys, low_values, high_keys, high_values):
        below = position - (turn + 1)
        above = position + (turn + 1)
        rows = jnp.concatenate([below * local_rows + local_range, above * local_rows + local_range])
        usable = jnp.concatenate(
            [
                jnp.broadcast_to(below >= 0, (local_rows,)),
                jnp.broadcast_to(above < ctx_count, (local_rows,)),
            ]
        )
        both_keys = jnp.concatenate([low_keys, high_keys], axis=0)
        both_values = jnp.concatenate([low_values, high_values], axis=0)
        return consume(state, both_keys, both_values, rows, usable)

    state = consume(initial, keys, values, query_rows, jnp.ones((local_rows,), jnp.bool_))
    reach = ctx_count // 4

    def travel(turn, carry):
        state, low_keys, low_values, high_keys, high_values = carry
        low_keys, low_values = shifted((low_keys, low_values), "ctx", 1)
        high_keys, high_values = shifted((high_keys, high_values), "ctx", -1)
        state = remote(state, turn, low_keys, low_values, high_keys, high_values)
        return (state, low_keys, low_values, high_keys, high_values)

    state = lax.fori_loop(0, reach, travel, (state, keys, values, keys, values))[0]
    running_max, running_sum, numerator = state
    result = numerator / running_sum[:, :, None]
    return (
        jnp.transpose(result, (1, 0, 2)).reshape(local_rows, head_count * DH).astype(jnp.bfloat16)
    )


def solution(mesh):
    placed = (P("ctx", "head"), P("ctx", None), P("ctx", None), P(), P())
    return jax.shard_map(
        body, mesh=mesh, in_specs=placed, out_specs=P("ctx", "head"), check_vma=False
    )
```

profile of v0, /device:TPU:48, one launch (start us, length us, event | category | flops | bytes accessed | tf_op | source)
XLA Modules:
  0.0 540.1 jit_solution(13605586332287585277)
XLA Ops:
  6.0 533.3 %while.29 = (s32[]{:T(128)}, f32[1,512]{1,0:T(1,128)S(1)}, f32[1,512]{1,0:T(1,128)S(1)}, f32[1,512,128]{2,1,0:T(8,128)S(1)}, bf16[512,128]{1,0:T(8,128)(2,1)S(1)...) while((s32[]{:T(128)}, f32[1,512]{1,0:T(1,128)S(1)}, ...), condition=%wide.region_10.11_spmd.clone.clone, body=%wide.region_5.10_spmd.clone.clone.sunk | while | flops 283195392 | bytes 10733521 | solution.py:97
  6.0 14.5 %collective-permute-start = (bf16[512,128]{1,0:T(8,128)(2,1)S(1)}, bf16[512,128]{1,0:T(8,128)(2,1)S(1)}, u32[]{:S(2)}, u32[]{:S(2)}) collective-permute-start(bf16[512,128]{1,0:T(8,128)(2,1)S(1)} %get-tuple-element.589), channel_id=1, source_target_pairs={{8,0},{16,8},{24,16},{32,24},{40,32},{48,40},{56,48},{64,56},{72,6... | collective-permute-start | bytes 393224 | tf_op jit(solution)/shard_map/while/body/eval_jaxpr/ppermute | solution.py:17
  22.4 12.0 %collective-permute-start.2 = (bf16[512,128]{1,0:T(8,128)(2,1)S(1)}, bf16[512,128]{1,0:T(8,128)(2,1)S(1)}, u32[]{:S(2)}, u32[]{:S(2)}) collective-permute-start(bf16[512,128]{1,0:T(8,128)(2,1)S(1)} %get-tuple-element.590), channel_id=1, source_target_pairs={{8,0},{16,8},{24,16},{32,24},{40,32},{48,40},{56,48},{64,56},{72,6... | collective-permute-start | bytes 393224 | tf_op jit(solution)/shard_map/while/body/eval_jaxpr/ppermute | solution.py:17
  40.2 11.2 %collective-permute-done.3 = bf16[512,128]{1,0:T(8,128)(2,1)S(1)} collective-permute-done((bf16[512,128]{1,0:T(8,128)(2,1)S(1)}, bf16[512,128]{1,0:T(8,128)(2,1)S(1)}, u32[]{:S(2)}, u32[]{:S(2)}) %collective-permute-start.3) | collective-permute-done | bytes 131104 | tf_op jit(solution)/shard_map/while/body/eval_jaxpr/ppermute | solution.py:17
  58.7 10.0 %collective-permute-start.2 = (bf16[512,128]{1,0:T(8,128)(2,1)S(1)}, bf16[512,128]{1,0:T(8,128)(2,1)S(1)}, u32[]{:S(2)}, u32[]{:S(2)}) collective-permute-start(bf16[512,128]{1,0:T(8,128)(2,1)S(1)} %get-tuple-element.590), channel_id=1, source_target_pairs={{8,0},{16,8},{24,16},{32,24},{40,32},{48,40},{56,48},{64,56},{72,6... | collective-permute-start | bytes 393224 | tf_op jit(solution)/shard_map/while/body/eval_jaxpr/ppermute | solution.py:17
  73.4 11.0 %collective-permute-done.3 = bf16[512,128]{1,0:T(8,128)(2,1)S(1)} collective-permute-done((bf16[512,128]{1,0:T(8,128)(2,1)S(1)}, bf16[512,128]{1,0:T(8,128)(2,1)S(1)}, u32[]{:S(2)}, u32[]{:S(2)}) %collective-permute-start.3) | collective-permute-done | bytes 131104 | tf_op jit(solution)/shard_map/while/body/eval_jaxpr/ppermute | solution.py:17
  91.6 10.0 %collective-permute-start.2 = (bf16[512,128]{1,0:T(8,128)(2,1)S(1)}, bf16[512,128]{1,0:T(8,128)(2,1)S(1)}, u32[]{:S(2)}, u32[]{:S(2)}) collective-permute-start(bf16[512,128]{1,0:T(8,128)(2,1)S(1)} %get-tuple-element.590), channel_id=1, source_target_pairs={{8,0},{16,8},{24,16},{32,24},{40,32},{48,40},{56,48},{64,56},{72,6... | collective-permute-start | bytes 393224 | tf_op jit(solution)/shard_map/while/body/eval_jaxpr/ppermute | solution.py:17
  106.4 10.4 %collective-permute-done.3 = bf16[512,128]{1,0:T(8,128)(2,1)S(1)} collective-permute-done((bf16[512,128]{1,0:T(8,128)(2,1)S(1)}, bf16[512,128]{1,0:T(8,128)(2,1)S(1)}, u32[]{:S(2)}, u32[]{:S(2)}) %collective-permute-start.3) | collective-permute-done | bytes 131104 | tf_op jit(solution)/shard_map/while/body/eval_jaxpr/ppermute | solution.py:17
  124.0 10.0 %collective-permute-start.2 = (bf16[512,128]{1,0:T(8,128)(2,1)S(1)}, bf16[512,128]{1,0:T(8,128)(2,1)S(1)}, u32[]{:S(2)}, u32[]{:S(2)}) collective-permute-start(bf16[512,128]{1,0:T(8,128)(2,1)S(1)} %get-tuple-element.590), channel_id=1, source_target_pairs={{8,0},{16,8},{24,16},{32,24},{40,32},{48,40},{56,48},{64,56},{72,6... | collective-permute-start | bytes 393224 | tf_op jit(solution)/shard_map/while/body/eval_jaxpr/ppermute | solution.py:17
  138.7 10.4 %collective-permute-done.3 = bf16[512,128]{1,0:T(8,128)(2,1)S(1)} collective-permute-done((bf16[512,128]{1,0:T(8,128)(2,1)S(1)}, bf16[512,128]{1,0:T(8,128)(2,1)S(1)}, u32[]{:S(2)}, u32[]{:S(2)}) %collective-permute-start.3) | collective-permute-done | bytes 131104 | tf_op jit(solution)/shard_map/while/body/eval_jaxpr/ppermute | solution.py:17
  156.3 10.0 %collective-permute-start.2 = (bf16[512,128]{1,0:T(8,128)(2,1)S(1)}, bf16[512,128]{1,0:T(8,128)(2,1)S(1)}, u32[]{:S(2)}, u32[]{:S(2)}) collective-permute-start(bf16[512,128]{1,0:T(8,128)(2,1)S(1)} %get-tuple-element.590), channel_id=1, source_target_pairs={{8,0},{16,8},{24,16},{32,24},{40,32},{48,40},{56,48},{64,56},{72,6... | collective-permute-start | bytes 393224 | tf_op jit(solution)/shard_map/while/body/eval_jaxpr/ppermute | solution.py:17
  171.1 10.4 %collective-permute-done.3 = bf16[512,128]{1,0:T(8,128)(2,1)S(1)} collective-permute-done((bf16[512,128]{1,0:T(8,128)(2,1)S(1)}, bf16[512,128]{1,0:T(8,128)(2,1)S(1)}, u32[]{:S(2)}, u32[]{:S(2)}) %collective-permute-start.3) | collective-permute-done | bytes 131104 | tf_op jit(solution)/shard_map/while/body/eval_jaxpr/ppermute | solution.py:17
  188.7 10.0 %collective-permute-start.2 = (bf16[512,128]{1,0:T(8,128)(2,1)S(1)}, bf16[512,128]{1,0:T(8,128)(2,1)S(1)}, u32[]{:S(2)}, u32[]{:S(2)}) collective-permute-start(bf16[512,128]{1,0:T(8,128)(2,1)S(1)} %get-tuple-element.590), channel_id=1, source_target_pairs={{8,0},{16,8},{24,16},{32,24},{40,32},{48,40},{56,48},{64,56},{72,6... | collective-permute-start | bytes 393224 | tf_op jit(solution)/shard_map/while/body/eval_jaxpr/ppermute | solution.py:17
  203.4 10.4 %collective-permute-done.3 = bf16[512,128]{1,0:T(8,128)(2,1)S(1)} collective-permute-done((bf16[512,128]{1,0:T(8,128)(2,1)S(1)}, bf16[512,128]{1,0:T(8,128)(2,1)S(1)}, u32[]{:S(2)}, u32[]{:S(2)}) %collective-permute-start.3) | collective-permute-done | bytes 131104 | tf_op jit(solution)/shard_map/while/body/eval_jaxpr/ppermute | solution.py:17
  221.0 10.0 %collective-permute-start.2 = (bf16[512,128]{1,0:T(8,128)(2,1)S(1)}, bf16[512,128]{1,0:T(8,128)(2,1)S(1)}, u32[]{:S(2)}, u32[]{:S(2)}) collective-permute-start(bf16[512,128]{1,0:T(8,128)(2,1)S(1)} %get-tuple-element.590), channel_id=1, source_target_pairs={{8,0},{16,8},{24,16},{32,24},{40,32},{48,40},{56,48},{64,56},{72,6... | collective-permute-start | bytes 393224 | tf_op jit(solution)/shard_map/while/body/eval_jaxpr/ppermute | solution.py:17
  235.8 10.3 %collective-permute-done.3 = bf16[512,128]{1,0:T(8,128)(2,1)S(1)} collective-permute-done((bf16[512,128]{1,0:T(8,128)(2,1)S(1)}, bf16[512,128]{1,0:T(8,128)(2,1)S(1)}, u32[]{:S(2)}, u32[]{:S(2)}) %collective-permute-start.3) | collective-permute-done | bytes 131104 | tf_op jit(solution)/shard_map/while/body/eval_jaxpr/ppermute | solution.py:17
  253.3 10.0 %collective-permute-start.2 = (bf16[512,128]{1,0:T(8,128)(2,1)S(1)}, bf16[512,128]{1,0:T(8,128)(2,1)S(1)}, u32[]{:S(2)}, u32[]{:S(2)}) collective-permute-start(bf16[512,128]{1,0:T(8,128)(2,1)S(1)} %get-tuple-element.590), channel_id=1, source_target_pairs={{8,0},{16,8},{24,16},{32,24},{40,32},{48,40},{56,48},{64,56},{72,6... | collective-permute-start | bytes 393224 | tf_op jit(solution)/shard_map/while/body/eval_jaxpr/ppermute | solution.py:17
  268.2 10.2 %collective-permute-done.3 = bf16[512,128]{1,0:T(8,128)(2,1)S(1)} collective-permute-done((bf16[512,128]{1,0:T(8,128)(2,1)S(1)}, bf16[512,128]{1,0:T(8,128)(2,1)S(1)}, u32[]{:S(2)}, u32[]{:S(2)}) %collective-permute-start.3) | collective-permute-done | bytes 131104 | tf_op jit(solution)/shard_map/while/body/eval_jaxpr/ppermute | solution.py:17
  285.6 10.0 %collective-permute-start.2 = (bf16[512,128]{1,0:T(8,128)(2,1)S(1)}, bf16[512,128]{1,0:T(8,128)(2,1)S(1)}, u32[]{:S(2)}, u32[]{:S(2)}) collective-permute-start(bf16[512,128]{1,0:T(8,128)(2,1)S(1)} %get-tuple-element.590), channel_id=1, source_target_pairs={{8,0},{16,8},{24,16},{32,24},{40,32},{48,40},{56,48},{64,56},{72,6... | collective-permute-start | bytes 393224 | tf_op jit(solution)/shard_map/while/body/eval_jaxpr/ppermute | solution.py:17
  300.6 10.1 %collective-permute-done.3 = bf16[512,128]{1,0:T(8,128)(2,1)S(1)} collective-permute-done((bf16[512,128]{1,0:T(8,128)(2,1)S(1)}, bf16[512,128]{1,0:T(8,128)(2,1)S(1)}, u32[]{:S(2)}, u32[]{:S(2)}) %collective-permute-start.3) | collective-permute-done | bytes 131104 | tf_op jit(solution)/shard_map/while/body/eval_jaxpr/ppermute | solution.py:17
  317.9 10.0 %collective-permute-start.2 = (bf16[512,128]{1,0:T(8,128)(2,1)S(1)}, bf16[512,128]{1,0:T(8,128)(2,1)S(1)}, u32[]{:S(2)}, u32[]{:S(2)}) collective-permute-start(bf16[512,128]{1,0:T(8,128)(2,1)S(1)} %get-tuple-element.590), channel_id=1, source_target_pairs={{8,0},{16,8},{24,16},{32,24},{40,32},{48,40},{56,48},{64,56},{72,6... | collective-permute-start | bytes 393224 | tf_op jit(solution)/shard_map/while/body/eval_jaxpr/ppermute | solution.py:17
  332.6 10.3 %collective-permute-done.3 = bf16[512,128]{1,0:T(8,128)(2,1)S(1)} collective-permute-done((bf16[512,128]{1,0:T(8,128)(2,1)S(1)}, bf16[512,128]{1,0:T(8,128)(2,1)S(1)}, u32[]{:S(2)}, u32[]{:S(2)}) %collective-permute-start.3) | collective-permute-done | bytes 131104 | tf_op jit(solution)/shard_map/while/body/eval_jaxpr/ppermute | solution.py:17
  350.2 10.0 %collective-permute-start.2 = (bf16[512,128]{1,0:T(8,128)(2,1)S(1)}, bf16[512,128]{1,0:T(8,128)(2,1)S(1)}, u32[]{:S(2)}, u32[]{:S(2)}) collective-permute-start(bf16[512,128]{1,0:T(8,128)(2,1)S(1)} %get-tuple-element.590), channel_id=1, source_target_pairs={{8,0},{16,8},{24,16},{32,24},{40,32},{48,40},{56,48},{64,56},{72,6... | collective-permute-start | bytes 393224 | tf_op jit(solution)/shard_map/while/body/eval_jaxpr/ppermute | solution.py:17
  364.9 11.7 %collective-permute-done.3 = bf16[512,128]{1,0:T(8,128)(2,1)S(1)} collective-permute-done((bf16[512,128]{1,0:T(8,128)(2,1)S(1)}, bf16[512,128]{1,0:T(8,128)(2,1)S(1)}, u32[]{:S(2)}, u32[]{:S(2)}) %collective-permute-start.3) | collective-permute-done | bytes 131104 | tf_op jit(solution)/shard_map/while/body/eval_jaxpr/ppermute | solution.py:17
  383.8 10.0 %collective-permute-start.2 = (bf16[512,128]{1,0:T(8,128)(2,1)S(1)}, bf16[512,128]{1,0:T(8,128)(2,1)S(1)}, u32[]{:S(2)}, u32[]{:S(2)}) collective-permute-start(bf16[512,128]{1,0:T(8,128)(2,1)S(1)} %get-tuple-element.590), channel_id=1, source_target_pairs={{8,0},{16,8},{24,16},{32,24},{40,32},{48,40},{56,48},{64,56},{72,6... | collective-permute-start | bytes 393224 | tf_op jit(solution)/shard_map/while/body/eval_jaxpr/ppermute | solution.py:17
  398.6 10.3 %collective-permute-done.3 = bf16[512,128]{1,0:T(8,128)(2,1)S(1)} collective-permute-done((bf16[512,128]{1,0:T(8,128)(2,1)S(1)}, bf16[512,128]{1,0:T(8,128)(2,1)S(1)}, u32[]{:S(2)}, u32[]{:S(2)}) %collective-permute-start.3) | collective-permute-done | bytes 131104 | tf_op jit(solution)/shard_map/while/body/eval_jaxpr/ppermute | solution.py:17
  416.1 10.0 %collective-permute-start.2 = (bf16[512,128]{1,0:T(8,128)(2,1)S(1)}, bf16[512,128]{1,0:T(8,128)(2,1)S(1)}, u32[]{:S(2)}, u32[]{:S(2)}) collective-permute-start(bf16[512,128]{1,0:T(8,128)(2,1)S(1)} %get-tuple-element.590), channel_id=1, source_target_pairs={{8,0},{16,8},{24,16},{32,24},{40,32},{48,40},{56,48},{64,56},{72,6... | collective-permute-start | bytes 393224 | tf_op jit(solution)/shard_map/while/body/eval_jaxpr/ppermute | solution.py:17
  430.9 10.3 %collective-permute-done.3 = bf16[512,128]{1,0:T(8,128)(2,1)S(1)} collective-permute-done((bf16[512,128]{1,0:T(8,128)(2,1)S(1)}, bf16[512,128]{1,0:T(8,128)(2,1)S(1)}, u32[]{:S(2)}, u32[]{:S(2)}) %collective-permute-start.3) | collective-permute-done | bytes 131104 | tf_op jit(solution)/shard_map/while/body/eval_jaxpr/ppermute | solution.py:17
  448.4 10.0 %collective-permute-start.2 = (bf16[512,128]{1,0:T(8,128)(2,1)S(1)}, bf16[512,128]{1,0:T(8,128)(2,1)S(1)}, u32[]{:S(2)}, u32[]{:S(2)}) collective-permute-start(bf16[512,128]{1,0:T(8,128)(2,1)S(1)} %get-tuple-element.590), channel_id=1, source_target_pairs={{8,0},{16,8},{24,16},{32,24},{40,32},{48,40},{56,48},{64,56},{72,6... | collective-permute-start | bytes 393224 | tf_op jit(solution)/shard_map/while/body/eval_jaxpr/ppermute | solution.py:17
  463.1 10.3 %collective-permute-done.3 = bf16[512,128]{1,0:T(8,128)(2,1)S(1)} collective-permute-done((bf16[512,128]{1,0:T(8,128)(2,1)S(1)}, bf16[512,128]{1,0:T(8,128)(2,1)S(1)}, u32[]{:S(2)}, u32[]{:S(2)}) %collective-permute-start.3) | collective-permute-done | bytes 131104 | tf_op jit(solution)/shard_map/while/body/eval_jaxpr/ppermute | solution.py:17
  495.4 10.3 %collective-permute-done.3 = bf16[512,128]{1,0:T(8,128)(2,1)S(1)} collective-permute-done((bf16[512,128]{1,0:T(8,128)(2,1)S(1)}, bf16[512,128]{1,0:T(8,128)(2,1)S(1)}, u32[]{:S(2)}, u32[]{:S(2)}) %collective-permute-start.3) | collective-permute-done | bytes 131104 | tf_op jit(solution)/shard_map/while/body/eval_jaxpr/ppermute | solution.py:17
  527.6 10.3 %collective-permute-done.3 = bf16[512,128]{1,0:T(8,128)(2,1)S(1)} collective-permute-done((bf16[512,128]{1,0:T(8,128)(2,1)S(1)}, bf16[512,128]{1,0:T(8,128)(2,1)S(1)}, u32[]{:S(2)}, u32[]{:S(2)}) %collective-permute-start.3) | collective-permute-done | bytes 131104 | tf_op jit(solution)/shard_map/while/body/eval_jaxpr/ppermute | solution.py:17
  (390 shorter events, 212.1 us)
Async XLA Ops:
  6.0 31.0 %collective-permute-start = (bf16[512,128]{1,0:T(8,128)(2,1)S(1)}, bf16[512,128]{1,0:T(8,128)(2,1)S(1)}, u32[]{:S(2)}, u32[]{:S(2)}) collective-permute-start(bf16[512,128]{1,0:T(8,128)(2,1)S(1)} %get-tuple-element.589), channel_id=1, source_target_pairs={{8,0},{16,8},{24,16},{32,24},{40,32},{48,40},{56,48},{64,56},{72,6... | collective-permute-start | bytes 393224 | tf_op jit(solution)/shard_map/while/body/eval_jaxpr/ppermute | solution.py:17
  22.4 29.1 %collective-permute-start.2 = (bf16[512,128]{1,0:T(8,128)(2,1)S(1)}, bf16[512,128]{1,0:T(8,128)(2,1)S(1)}, u32[]{:S(2)}, u32[]{:S(2)}) collective-permute-start(bf16[512,128]{1,0:T(8,128)(2,1)S(1)} %get-tuple-element.590), channel_id=1, source_target_pairs={{8,0},{16,8},{24,16},{32,24},{40,32},{48,40},{56,48},{64,56},{72,6... | collective-permute-start | bytes 393224 | tf_op jit(solution)/shard_map/while/body/eval_jaxpr/ppermute | solution.py:17
  52.8 18.4 %collective-permute-start = (bf16[512,128]{1,0:T(8,128)(2,1)S(1)}, bf16[512,128]{1,0:T(8,128)(2,1)S(1)}, u32[]{:S(2)}, u32[]{:S(2)}) collective-permute-start(bf16[512,128]{1,0:T(8,128)(2,1)S(1)} %get-tuple-element.589), channel_id=1, source_target_pairs={{8,0},{16,8},{24,16},{32,24},{40,32},{48,40},{56,48},{64,56},{72,6... | collective-permute-start | bytes 393224 | tf_op jit(solution)/shard_map/while/body/eval_jaxpr/ppermute | solution.py:17
  58.7 25.7 %collective-permute-start.2 = (bf16[512,128]{1,0:T(8,128)(2,1)S(1)}, bf16[512,128]{1,0:T(8,128)(2,1)S(1)}, u32[]{:S(2)}, u32[]{:S(2)}) collective-permute-start(bf16[512,128]{1,0:T(8,128)(2,1)S(1)} %get-tuple-element.590), channel_id=1, source_target_pairs={{8,0},{16,8},{24,16},{32,24},{40,32},{48,40},{56,48},{64,56},{72,6... | collective-permute-start | bytes 393224 | tf_op jit(solution)/shard_map/while/body/eval_jaxpr/ppermute | solution.py:17
  85.8 18.4 %collective-permute-start = (bf16[512,128]{1,0:T(8,128)(2,1)S(1)}, bf16[512,128]{1,0:T(8,128)(2,1)S(1)}, u32[]{:S(2)}, u32[]{:S(2)}) collective-permute-start(bf16[512,128]{1,0:T(8,128)(2,1)S(1)} %get-tuple-element.589), channel_id=1, source_target_pairs={{8,0},{16,8},{24,16},{32,24},{40,32},{48,40},{56,48},{64,56},{72,6... | collective-permute-start | bytes 393224 | tf_op jit(solution)/shard_map/while/body/eval_jaxpr/ppermute | solution.py:17
  91.6 25.2 %collective-permute-start.2 = (bf16[512,128]{1,0:T(8,128)(2,1)S(1)}, bf16[512,128]{1,0:T(8,128)(2,1)S(1)}, u32[]{:S(2)}, u32[]{:S(2)}) collective-permute-start(bf16[512,128]{1,0:T(8,128)(2,1)S(1)} %get-tuple-element.590), channel_id=1, source_target_pairs={{8,0},{16,8},{24,16},{32,24},{40,32},{48,40},{56,48},{64,56},{72,6... | collective-permute-start | bytes 393224 | tf_op jit(solution)/shard_map/while/body/eval_jaxpr/ppermute | solution.py:17
  118.1 18.4 %collective-permute-start = (bf16[512,128]{1,0:T(8,128)(2,1)S(1)}, bf16[512,128]{1,0:T(8,128)(2,1)S(1)}, u32[]{:S(2)}, u32[]{:S(2)}) collective-permute-start(bf16[512,128]{1,0:T(8,128)(2,1)S(1)} %get-tuple-element.589), channel_id=1, source_target_pairs={{8,0},{16,8},{24,16},{32,24},{40,32},{48,40},{56,48},{64,56},{72,6... | collective-permute-start | bytes 393224 | tf_op jit(solution)/shard_map/while/body/eval_jaxpr/ppermute | solution.py:17
  124.0 25.1 %collective-permute-start.2 = (bf16[512,128]{1,0:T(8,128)(2,1)S(1)}, bf16[512,128]{1,0:T(8,128)(2,1)S(1)}, u32[]{:S(2)}, u32[]{:S(2)}) collective-permute-start(bf16[512,128]{1,0:T(8,128)(2,1)S(1)} %get-tuple-element.590), channel_id=1, source_target_pairs={{8,0},{16,8},{24,16},{32,24},{40,32},{48,40},{56,48},{64,56},{72,6... | collective-permute-start | bytes 393224 | tf_op jit(solution)/shard_map/while/body/eval_jaxpr/ppermute | solution.py:17
  150.5 18.4 %collective-permute-start = (bf16[512,128]{1,0:T(8,128)(2,1)S(1)}, bf16[512,128]{1,0:T(8,128)(2,1)S(1)}, u32[]{:S(2)}, u32[]{:S(2)}) collective-permute-start(bf16[512,128]{1,0:T(8,128)(2,1)S(1)} %get-tuple-element.589), channel_id=1, source_target_pairs={{8,0},{16,8},{24,16},{32,24},{40,32},{48,40},{56,48},{64,56},{72,6... | collective-permute-start | bytes 393224 | tf_op jit(solution)/shard_map/while/body/eval_jaxpr/ppermute | solution.py:17
  156.3 25.1 %collective-permute-start.2 = (bf16[512,128]{1,0:T(8,128)(2,1)S(1)}, bf16[512,128]{1,0:T(8,128)(2,1)S(1)}, u32[]{:S(2)}, u32[]{:S(2)}) collective-permute-start(bf16[512,128]{1,0:T(8,128)(2,1)S(1)} %get-tuple-element.590), channel_id=1, source_target_pairs={{8,0},{16,8},{24,16},{32,24},{40,32},{48,40},{56,48},{64,56},{72,6... | collective-permute-start | bytes 393224 | tf_op jit(solution)/shard_map/while/body/eval_jaxpr/ppermute | solution.py:17
  182.8 18.4 %collective-permute-start = (bf16[512,128]{1,0:T(8,128)(2,1)S(1)}, bf16[512,128]{1,0:T(8,128)(2,1)S(1)}, u32[]{:S(2)}, u32[]{:S(2)}) collective-permute-start(bf16[512,128]{1,0:T(8,128)(2,1)S(1)} %get-tuple-element.589), channel_id=1, source_target_pairs={{8,0},{16,8},{24,16},{32,24},{40,32},{48,40},{56,48},{64,56},{72,6... | collective-permute-start | bytes 393224 | tf_op jit(solution)/shard_map/while/body/eval_jaxpr/ppermute | solution.py:17
  188.7 25.1 %collective-permute-start.2 = (bf16[512,128]{1,0:T(8,128)(2,1)S(1)}, bf16[512,128]{1,0:T(8,128)(2,1)S(1)}, u32[]{:S(2)}, u32[]{:S(2)}) collective-permute-start(bf16[512,128]{1,0:T(8,128)(2,1)S(1)} %get-tuple-element.590), channel_id=1, source_target_pairs={{8,0},{16,8},{24,16},{32,24},{40,32},{48,40},{56,48},{64,56},{72,6... | collective-permute-start | bytes 393224 | tf_op jit(solution)/shard_map/while/body/eval_jaxpr/ppermute | solution.py:17
  215.1 18.4 %collective-permute-start = (bf16[512,128]{1,0:T(8,128)(2,1)S(1)}, bf16[512,128]{1,0:T(8,128)(2,1)S(1)}, u32[]{:S(2)}, u32[]{:S(2)}) collective-permute-start(bf16[512,128]{1,0:T(8,128)(2,1)S(1)} %get-tuple-element.589), channel_id=1, source_target_pairs={{8,0},{16,8},{24,16},{32,24},{40,32},{48,40},{56,48},{64,56},{72,6... | collective-permute-start | bytes 393224 | tf_op jit(solution)/shard_map/while/body/eval_jaxpr/ppermute | solution.py:17
  221.0 25.1 %collective-permute-start.2 = (bf16[512,128]{1,0:T(8,128)(2,1)S(1)}, bf16[512,128]{1,0:T(8,128)(2,1)S(1)}, u32[]{:S(2)}, u32[]{:S(2)}) collective-permute-start(bf16[512,128]{1,0:T(8,128)(2,1)S(1)} %get-tuple-element.590), channel_id=1, source_target_pairs={{8,0},{16,8},{24,16},{32,24},{40,32},{48,40},{56,48},{64,56},{72,6... | collective-permute-start | bytes 393224 | tf_op jit(solution)/shard_map/while/body/eval_jaxpr/ppermute | solution.py:17
  247.5 18.4 %collective-permute-start = (bf16[512,128]{1,0:T(8,128)(2,1)S(1)}, bf16[512,128]{1,0:T(8,128)(2,1)S(1)}, u32[]{:S(2)}, u32[]{:S(2)}) collective-permute-start(bf16[512,128]{1,0:T(8,128)(2,1)S(1)} %get-tuple-element.589), channel_id=1, source_target_pairs={{8,0},{16,8},{24,16},{32,24},{40,32},{48,40},{56,48},{64,56},{72,6... | collective-permute-start | bytes 393224 | tf_op jit(solution)/shard_map/while/body/eval_jaxpr/ppermute | solution.py:17
  253.3 25.1 %collective-permute-start.2 = (bf16[512,128]{1,0:T(8,128)(2,1)S(1)}, bf16[512,128]{1,0:T(8,128)(2,1)S(1)}, u32[]{:S(2)}, u32[]{:S(2)}) collective-permute-start(bf16[512,128]{1,0:T(8,128)(2,1)S(1)} %get-tuple-element.590), channel_id=1, source_target_pairs={{8,0},{16,8},{24,16},{32,24},{40,32},{48,40},{56,48},{64,56},{72,6... | collective-permute-start | bytes 393224 | tf_op jit(solution)/shard_map/while/body/eval_jaxpr/ppermute | solution.py:17
  279.8 18.4 %collective-permute-start = (bf16[512,128]{1,0:T(8,128)(2,1)S(1)}, bf16[512,128]{1,0:T(8,128)(2,1)S(1)}, u32[]{:S(2)}, u32[]{:S(2)}) collective-permute-start(bf16[512,128]{1,0:T(8,128)(2,1)S(1)} %get-tuple-element.589), channel_id=1, source_target_pairs={{8,0},{16,8},{24,16},{32,24},{40,32},{48,40},{56,48},{64,56},{72,6... | collective-permute-start | bytes 393224 | tf_op jit(solution)/shard_map/while/body/eval_jaxpr/ppermute | solution.py:17
  285.6 25.1 %collective-permute-start.2 = (bf16[512,128]{1,0:T(8,128)(2,1)S(1)}, bf16[512,128]{1,0:T(8,128)(2,1)S(1)}, u32[]{:S(2)}, u32[]{:S(2)}) collective-permute-start(bf16[512,128]{1,0:T(8,128)(2,1)S(1)} %get-tuple-element.590), channel_id=1, source_target_pairs={{8,0},{16,8},{24,16},{32,24},{40,32},{48,40},{56,48},{64,56},{72,6... | collective-permute-start | bytes 393224 | tf_op jit(solution)/shard_map/while/body/eval_jaxpr/ppermute | solution.py:17
  312.0 18.4 %collective-permute-start = (bf16[512,128]{1,0:T(8,128)(2,1)S(1)}, bf16[512,128]{1,0:T(8,128)(2,1)S(1)}, u32[]{:S(2)}, u32[]{:S(2)}) collective-permute-start(bf16[512,128]{1,0:T(8,128)(2,1)S(1)} %get-tuple-element.589), channel_id=1, source_target_pairs={{8,0},{16,8},{24,16},{32,24},{40,32},{48,40},{56,48},{64,56},{72,6... | collective-permute-start | bytes 393224 | tf_op jit(solution)/shard_map/while/body/eval_jaxpr/ppermute | solution.py:17
  317.9 25.1 %collective-permute-start.2 = (bf16[512,128]{1,0:T(8,128)(2,1)S(1)}, bf16[512,128]{1,0:T(8,128)(2,1)S(1)}, u32[]{:S(2)}, u32[]{:S(2)}) collective-permute-start(bf16[512,128]{1,0:T(8,128)(2,1)S(1)} %get-tuple-element.590), channel_id=1, source_target_pairs={{8,0},{16,8},{24,16},{32,24},{40,32},{48,40},{56,48},{64,56},{72,6... | collective-permute-start | bytes 393224 | tf_op jit(solution)/shard_map/while/body/eval_jaxpr/ppermute | solution.py:17
  344.3 18.4 %collective-permute-start = (bf16[512,128]{1,0:T(8,128)(2,1)S(1)}, bf16[512,128]{1,0:T(8,128)(2,1)S(1)}, u32[]{:S(2)}, u32[]{:S(2)}) collective-permute-start(bf16[512,128]{1,0:T(8,128)(2,1)S(1)} %get-tuple-element.589), channel_id=1, source_target_pairs={{8,0},{16,8},{24,16},{32,24},{40,32},{48,40},{56,48},{64,56},{72,6... | collective-permute-start | bytes 393224 | tf_op jit(solution)/shard_map/while/body/eval_jaxpr/ppermute | solution.py:17
  350.2 26.5 %collective-permute-start.2 = (bf16[512,128]{1,0:T(8,128)(2,1)S(1)}, bf16[512,128]{1,0:T(8,128)(2,1)S(1)}, u32[]{:S(2)}, u32[]{:S(2)}) collective-permute-start(bf16[512,128]{1,0:T(8,128)(2,1)S(1)} %get-tuple-element.590), channel_id=1, source_target_pairs={{8,0},{16,8},{24,16},{32,24},{40,32},{48,40},{56,48},{64,56},{72,6... | collective-permute-start | bytes 393224 | tf_op jit(solution)/shard_map/while/body/eval_jaxpr/ppermute | solution.py:17
  378.0 18.4 %collective-permute-start = (bf16[512,128]{1,0:T(8,128)(2,1)S(1)}, bf16[512,128]{1,0:T(8,128)(2,1)S(1)}, u32[]{:S(2)}, u32[]{:S(2)}) collective-permute-start(bf16[512,128]{1,0:T(8,128)(2,1)S(1)} %get-tuple-element.589), channel_id=1, source_target_pairs={{8,0},{16,8},{24,16},{32,24},{40,32},{48,40},{56,48},{64,56},{72,6... | collective-permute-start | bytes 393224 | tf_op jit(solution)/shard_map/while/body/eval_jaxpr/ppermute | solution.py:17
  383.8 25.1 %collective-permute-start.2 = (bf16[512,128]{1,0:T(8,128)(2,1)S(1)}, bf16[512,128]{1,0:T(8,128)(2,1)S(1)}, u32[]{:S(2)}, u32[]{:S(2)}) collective-permute-start(bf16[512,128]{1,0:T(8,128)(2,1)S(1)} %get-tuple-element.590), channel_id=1, source_target_pairs={{8,0},{16,8},{24,16},{32,24},{40,32},{48,40},{56,48},{64,56},{72,6... | collective-permute-start | bytes 393224 | tf_op jit(solution)/shard_map/while/body/eval_jaxpr/ppermute | solution.py:17
  410.3 18.4 %collective-permute-start = (bf16[512,128]{1,0:T(8,128)(2,1)S(1)}, bf16[512,128]{1,0:T(8,128)(2,1)S(1)}, u32[]{:S(2)}, u32[]{:S(2)}) collective-permute-start(bf16[512,128]{1,0:T(8,128)(2,1)S(1)} %get-tuple-element.589), channel_id=1, source_target_pairs={{8,0},{16,8},{24,16},{32,24},{40,32},{48,40},{56,48},{64,56},{72,6... | collective-permute-start | bytes 393224 | tf_op jit(solution)/shard_map/while/body/eval_jaxpr/ppermute | solution.py:17
  416.1 25.1 %collective-permute-start.2 = (bf16[512,128]{1,0:T(8,128)(2,1)S(1)}, bf16[512,128]{1,0:T(8,128)(2,1)S(1)}, u32[]{:S(2)}, u32[]{:S(2)}) collective-permute-start(bf16[512,128]{1,0:T(8,128)(2,1)S(1)} %get-tuple-element.590), channel_id=1, source_target_pairs={{8,0},{16,8},{24,16},{32,24},{40,32},{48,40},{56,48},{64,56},{72,6... | collective-permute-start | bytes 393224 | tf_op jit(solution)/shard_map/while/body/eval_jaxpr/ppermute | solution.py:17
  442.5 18.4 %collective-permute-start = (bf16[512,128]{1,0:T(8,128)(2,1)S(1)}, bf16[512,128]{1,0:T(8,128)(2,1)S(1)}, u32[]{:S(2)}, u32[]{:S(2)}) collective-permute-start(bf16[512,128]{1,0:T(8,128)(2,1)S(1)} %get-tuple-element.589), channel_id=1, source_target_pairs={{8,0},{16,8},{24,16},{32,24},{40,32},{48,40},{56,48},{64,56},{72,6... | collective-permute-start | bytes 393224 | tf_op jit(solution)/shard_map/while/body/eval_jaxpr/ppermute | solution.py:17
  448.4 25.1 %collective-permute-start.2 = (bf16[512,128]{1,0:T(8,128)(2,1)S(1)}, bf16[512,128]{1,0:T(8,128)(2,1)S(1)}, u32[]{:S(2)}, u32[]{:S(2)}) collective-permute-start(bf16[512,128]{1,0:T(8,128)(2,1)S(1)} %get-tuple-element.590), channel_id=1, source_target_pairs={{8,0},{16,8},{24,16},{32,24},{40,32},{48,40},{56,48},{64,56},{72,6... | collective-permute-start | bytes 393224 | tf_op jit(solution)/shard_map/while/body/eval_jaxpr/ppermute | solution.py:17
  474.8 18.4 %collective-permute-start = (bf16[512,128]{1,0:T(8,128)(2,1)S(1)}, bf16[512,128]{1,0:T(8,128)(2,1)S(1)}, u32[]{:S(2)}, u32[]{:S(2)}) collective-permute-start(bf16[512,128]{1,0:T(8,128)(2,1)S(1)} %get-tuple-element.589), channel_id=1, source_target_pairs={{8,0},{16,8},{24,16},{32,24},{40,32},{48,40},{56,48},{64,56},{72,6... | collective-permute-start | bytes 393224 | tf_op jit(solution)/shard_map/while/body/eval_jaxpr/ppermute | solution.py:17
  480.6 25.1 %collective-permute-start.2 = (bf16[512,128]{1,0:T(8,128)(2,1)S(1)}, bf16[512,128]{1,0:T(8,128)(2,1)S(1)}, u32[]{:S(2)}, u32[]{:S(2)}) collective-permute-start(bf16[512,128]{1,0:T(8,128)(2,1)S(1)} %get-tuple-element.590), channel_id=1, source_target_pairs={{8,0},{16,8},{24,16},{32,24},{40,32},{48,40},{56,48},{64,56},{72,6... | collective-permute-start | bytes 393224 | tf_op jit(solution)/shard_map/while/body/eval_jaxpr/ppermute | solution.py:17
  507.1 18.4 %collective-permute-start = (bf16[512,128]{1,0:T(8,128)(2,1)S(1)}, bf16[512,128]{1,0:T(8,128)(2,1)S(1)}, u32[]{:S(2)}, u32[]{:S(2)}) collective-permute-start(bf16[512,128]{1,0:T(8,128)(2,1)S(1)} %get-tuple-element.589), channel_id=1, source_target_pairs={{8,0},{16,8},{24,16},{32,24},{40,32},{48,40},{56,48},{64,56},{72,6... | collective-permute-start | bytes 393224 | tf_op jit(solution)/shard_map/while/body/eval_jaxpr/ppermute | solution.py:17
  512.9 25.1 %collective-permute-start.2 = (bf16[512,128]{1,0:T(8,128)(2,1)S(1)}, bf16[512,128]{1,0:T(8,128)(2,1)S(1)}, u32[]{:S(2)}, u32[]{:S(2)}) collective-permute-start(bf16[512,128]{1,0:T(8,128)(2,1)S(1)} %get-tuple-element.590), channel_id=1, source_target_pairs={{8,0},{16,8},{24,16},{32,24},{40,32},{48,40},{56,48},{64,56},{72,6... | collective-permute-start | bytes 393224 | tf_op jit(solution)/shard_map/while/body/eval_jaxpr/ppermute | solution.py:17
  (34 other events, 511.3 us)
where the time goes:
time: 543 us; the launch traced here: 540 us
  starting transfers between devices  298 us (55%)
  waiting for transfers between devices  170 us (31%)
  matrix products  36.4 us (7%)
  other arithmetic  30.2 us (6%)
    ppermute x64, starting transfers between devices, shifted(): lax.ppermute(value, axis, [(source, source + steps) for source in range(l...  298 us
    ppermute x64, waiting for transfers between devices, shifted(): lax.ppermute(value, axis, [(source, source + steps) for source in range(l...  170 us
    dot_general x17, matrix products, absorb(): jnp.einsum('hts,sd->htd', weights.astype(jnp.bfloat16), value_block, pref...  21.4 us
    reduce_sum x17, other arithmetic, absorb(): running_sum = running_sum * factor + jnp.sum(weights, axis=2)  20.2 us
    dot_general x17, matrix products, absorb(): jnp.einsum('thd,sd->hts', query_heads, key_block, preferred_element_type=...  15 us
  transfers between devices with their start and end apart: 64, of which 20 were waited for; matrix products, arithmetic and copies ran while one was open for 8% of the time, Pallas kernels for 0%

commit v1 on v0

v1 whole, which is shorter than its diff:
```python
import functools
import math

import jax
import jax.numpy as jnp
from jax import lax
from jax.experimental import pallas as pl
from jax.experimental.pallas import tpu as pltpu
from jax.sharding import Mesh
from jax.sharding import PartitionSpec as P

DH = 128
CH = 256
AXES = ("y_hi", "z", "x", "y_lo", "core")
SIZES = (2, 8, 4, 4, 2)
CTX = AXES[:3]
HEAD = AXES[3:]
PLANES = SIZES[0] * SIZES[1]
EXTRA = 16
COEF = math.log2(math.e) / math.sqrt(DH)
NEGATIVE = -1e30
FLOOR = -1e25


def device(y_hi, z, x, y_lo, core):
    return (((y_hi * SIZES[1] + z) * SIZES[2] + x) * SIZES[3] + y_lo) * SIZES[4] + core


def plane_pairs(shift):
    pairs = []
    for plane in range(PLANES):
        for x in range(4):
            for y_lo in range(4):
                for core in range(2):
                    target = (plane if core == 0 else 2 * PLANES - 1 - plane) + shift
                    if target >= 2 * PLANES:
                        continue
                    folded = target >= PLANES
                    other = 2 * PLANES - 1 - target if folded else target
                    column = 3 - x if folded and core == 0 else x
                    row = y_lo if plane // 8 == other // 8 else 3 - y_lo
                    source = device(plane // 8, plane % 8, x, y_lo, core)
                    pairs.append((source, device(other // 8, other % 8, column, row, int(folded))))
    return pairs


def shifted(block, shift):
    return lax.ppermute(block, AXES, plane_pairs(shift))


def lower_slot(order_ref, ctx_ref):
    return jnp.where(order_ref[2 * ctx_ref[0]] == ctx_ref[0], 0, 1)


def pack_kernel(ctx_ref, core_ref, plane_ref, own_ref, order_ref, q_ref, k_ref, v_ref, qs_ref, kv_ref):
    low = lower_slot(order_ref, ctx_ref)
    own = jnp.where(core_ref[0] == 0, low, 1 - low)
    start = pl.multiple_of(own * CH, CH)
    kv_ref[:CH, :] = k_ref[pl.ds(start, CH), :]
    kv_ref[CH:, :] = v_ref[pl.ds(start, CH), :]
    for flow in range(2):
        slot = pl.multiple_of((low if flow == 0 else 1 - low) * CH, CH)
        block = q_ref[pl.ds(slot, CH), :]
        for x in range(4):
            qs_ref[2 * x + flow] = block


def limits_kernel(ctx_ref, core_ref, plane_ref, own_ref, length_ref, d_ref):
    rows = lax.broadcasted_iota(jnp.int32, (CH, 1), 0)
    lanes = lax.broadcasted_iota(jnp.int32, (CH, DH), 1)
    for column in range(4):
        place = rows + CH * (4 * plane_ref[0] + column)
        start = jnp.zeros((CH, 1), jnp.int32)
        end = jnp.int32(0)
        for doc in range(length_ref.shape[0]):
            end = end + length_ref[doc]
            start = jnp.where(place >= end, end, start)
        d_ref[column] = lanes - start


def attend_kernel(ctx_ref, core_ref, plane_ref, own_ref, q_ref, d_ref, kv0, kv1, kv2, kv34, o_ref, k_all, v_all):
    for slot, ref in enumerate((kv0, kv1, kv2, kv34.at[: 2 * CH], kv34.at[2 * CH :])):
        k_all[slot] = ref[:CH, :]
        v_all[slot, :, :DH] = ref[CH:, :]
        v_all[slot, :, DH:] = jnp.ones((CH, DH), jnp.bfloat16)
    core, plane, own = core_ref[0], plane_ref[0], own_ref[0]
    causal = lax.broadcasted_iota(jnp.int32, (CH, CH), 0) >= lax.broadcasted_iota(
        jnp.int32, (CH, CH), 1
    )
    eye = lax.broadcasted_iota(jnp.int32, (DH, DH), 0) == lax.broadcasted_iota(
        jnp.int32, (DH, DH), 1
    )
    extra_row = lax.broadcasted_iota(jnp.int32, (EXTRA, DH), 0)

    def one(turn, column, slots):
        x = jnp.where(core == 0, column, 3 - column)
        half = d_ref[column]
        d = jnp.concatenate([half, half + DH], axis=1)
        masks = []
        for slot in slots:
            mask = d >= -CH * (4 * (plane - slot) + own)
            if turn == 0 and isinstance(slot, int) and slot == 0:
                mask = mask & causal
            masks.append(mask)
        for head in range(2):
            block = 2 * x + head
            q = q_ref[block]
            scores = []
            top = None
            for slot, mask in zip(slots, masks):
                score = lax.dot_general(
                    q, k_all[slot], (((1,), (1,)), ((), ())), preferred_element_type=jnp.float32
                )
                score = jnp.where(mask, score, NEGATIVE)
                scores.append(score)
                top = score if top is None else jnp.maximum(top, score)
            top = jnp.maximum(jnp.max(top, axis=1, keepdims=True), FLOOR) * COEF
            total = None
            for slot, score in zip(slots, scores):
                weight = jnp.exp2(score * COEF - top).astype(jnp.bfloat16)
                term = jnp.dot(weight, v_all[slot], preferred_element_type=jnp.float32)
                total = term if total is None else total + term
            mass = total[:, DH:]
            o_ref[block, :CH, :] = (total[:, :DH] / jnp.maximum(mass, 1e-30)).astype(jnp.bfloat16)
            level = top + jnp.log2(jnp.maximum(mass, 1e-30))
            extra = jnp.zeros((EXTRA, DH), jnp.float32)
            for group in range(2):
                line = jnp.sum(
                    jnp.where(eye, level[group * DH : (group + 1) * DH], 0.0), axis=0, keepdims=True
                )
                for piece in range(3):
                    rounded = line.astype(jnp.bfloat16).astype(jnp.float32)
                    extra = jnp.where(extra_row == 2 * piece + group, rounded, extra)
                    line = line - rounded
            o_ref[block, CH:, :] = extra.astype(jnp.bfloat16)

    one(0, own, (0, 1, 2, 3, 4))
    for turn in range(1, 4):
        column = lax.rem(own + turn, 4)
        one(turn, column, (jnp.where(column > own, 0, 4), 1, 2, 3))


def merge_kernel(ctx_ref, core_ref, plane_ref, own_ref, order_ref, r_ref, out_ref, w_ref):
    low = lower_slot(order_ref, ctx_ref)
    w_ref[...] = jnp.zeros_like(w_ref)
    for flow in range(2):
        levels = []
        for x in range(4):
            pieces = r_ref[2 * x + flow, CH:, :].astype(jnp.float32)
            levels.append(pieces[0:2] + pieces[2:4] + pieces[4:6])
        top = functools.reduce(jnp.maximum, levels)
        shares = [jnp.exp2(level - top) for level in levels]
        total = functools.reduce(jnp.add, shares)
        for x in range(4):
            at = 8 * flow + 2 * x
            w_ref[at : at + 2, :] = shares[x] / total
    columns = w_ref[...].T
    for flow in range(2):
        slot = (low if flow == 0 else 1 - low) * CH
        for group in range(2):
            rows = slice(group * DH, (group + 1) * DH)
            total = None
            for x in range(4):
                at = 8 * flow + 2 * x + group
                term = columns[:, at : at + 1] * r_ref[2 * x + flow, rows, :].astype(jnp.float32)
                total = term if total is None else total + term
            start = pl.multiple_of(slot + group * DH, DH)
            out_ref[pl.ds(start, DH), :] = total.astype(jnp.bfloat16)


def in_vmem(count):
    return [pl.BlockSpec(memory_space=pltpu.VMEM)] * count


def in_smem(count):
    return [pl.BlockSpec(memory_space=pltpu.SMEM)] * count


def struct(shape, dtype=jnp.bfloat16):
    return jax.ShapeDtypeStruct(shape, dtype)


def close(array):
    return pltpu.with_memory_space_constraint(array, pltpu.VMEM)


def body(queries, keys, values, doc_lengths, span_order):
    ctx = lax.axis_index(CTX).astype(jnp.int32)
    core = lax.axis_index("core").astype(jnp.int32)
    first = core == 0
    z_line = jnp.where(first, ctx // 4, 2 * PLANES - 1 - ctx // 4)
    column = jnp.where(first, ctx % 4, 3 - ctx % 4)
    meta = tuple(part.reshape(1) for part in (ctx, core, z_line, column))

    sent, own = pl.pallas_call(
        pack_kernel,
        out_shape=(pltpu.VMEM((8, CH, DH), jnp.bfloat16), pltpu.VMEM((2 * CH, DH), jnp.bfloat16)),
        in_specs=in_smem(5) + in_vmem(3),
        out_specs=tuple(in_vmem(2)),
        name="pack",
    )(*meta, span_order, queries, keys, values)

    near = shifted(own, 1)
    two = shifted(own, 2)
    pair = shifted(jnp.concatenate([near, two]), 2)
    asked = lax.all_to_all(sent, ("x", "core"), 0, 0, tiled=True)

    limits = pl.pallas_call(
        limits_kernel,
        out_shape=pltpu.VMEM((4, CH, DH), jnp.int32),
        in_specs=in_smem(5),
        out_specs=in_vmem(1)[0],
        cost_estimate=pl.CostEstimate(flops=4000000, bytes_accessed=600000, transcendentals=0),
        name="limits",
    )(*meta, doc_lengths)

    partial = pl.pallas_call(
        attend_kernel,
        out_shape=pltpu.VMEM((8, CH + EXTRA, DH), jnp.bfloat16),
        in_specs=in_smem(4) + in_vmem(6),
        out_specs=in_vmem(1)[0],
        scratch_shapes=[
            pltpu.VMEM((5, CH, DH), jnp.bfloat16),
            pltpu.VMEM((5, CH, 2 * DH), jnp.bfloat16),
        ],
        name="attend",
    )(*meta, *map(close, (asked, limits, own, near, two, pair)))

    back = lax.all_to_all(partial, ("x", "core"), 0, 0, tiled=True)

    return pl.pallas_call(
        merge_kernel,
        out_shape=struct((2 * CH, DH)),
        in_specs=in_smem(5) + in_vmem(1),
        out_specs=in_vmem(1)[0],
        scratch_shapes=[pltpu.VMEM((DH, DH), jnp.float32)],
        name="merge",
    )(*meta, span_order, close(back))


def solution(mesh):
    parts = Mesh(mesh.devices.reshape(SIZES), AXES)
    placed = (P(CTX, HEAD), P(CTX, None), P(CTX, None), P(), P())
    return jax.shard_map(
        body, mesh=parts, in_specs=placed, out_specs=P(CTX, HEAD), check_vma=False
    )
```

time: 543 us -> 57.7 us (0.11)
  the two profiles are of different devices: /device:TPU:48 before, /device:TPU:41 now
where the time goes in v1:
time: 57.7 us; the launch traced here: 57.4 us
  starting transfers between devices  23.5 us (41%)
  blocking collectives  21.1 us (37%)
  Pallas kernels  8.88 us (15%)
  waiting for transfers between devices  3.84 us (7%)
    all_to_all x1, blocking collectives, body(): back = lax.all_to_all(partial, ('x', 'core'), 0, 0, tiled=True)  21.1 us
    ppermute x3, starting transfers between devices, shifted(): return lax.ppermute(block, AXES, plane_pairs(shift))  19.1 us
    all_to_all x1, starting transfers between devices, body(): asked = lax.all_to_all(sent, ('x', 'core'), 0, 0, tiled=True)  4.42 us
    pallas_call x1, Pallas kernels, body(): pl.pallas_call(attend_kernel, out_shape=pltpu.VMEM((8, CH + EXTRA, DH), j...  3.88 us
    ppermute x3, waiting for transfers between devices, shifted(): return lax.ppermute(block, AXES, plane_pairs(shift))  3.84 us
    pallas_call x1, Pallas kernels, body(): pl.pallas_call(pack_kernel, out_shape=(pltpu.VMEM((8, CH, DH), jnp.bfloat...  1.91 us
    pallas_call x1, Pallas kernels, body(): pl.pallas_call(merge_kernel, out_shape=struct((2 * CH, DH)), in_specs=in_...  1.84 us
    pallas_call x1, Pallas kernels, body(): pl.pallas_call(limits_kernel, out_shape=pltpu.VMEM((4, CH, DH), jnp.int32...  1.26 us
  transfers between devices with their start and end apart: 4, of which 1 were waited for; matrix products, arithmetic and copies ran while one was open for 0% of the time, Pallas kernels for 2%

profile of v1, /device:TPU:41, one launch (start us, length us, event | category | flops | bytes accessed | tf_op | source)
XLA Modules:
  0.0 57.4 jit_solution(17110233647307070854)
XLA Ops:
  0.0 1.9 %pack.1 = (bf16[8,256,128]{2,1,0:T(8,128)(2,1)}, bf16[512,128]{1,0:T(8,128)(2,1)S(1)}) custom-call(s32[1]{0:T(128)} %bitcast.ctx_ref, s32[1]{0:T(128)} %bitcast.1.core_ref, s32[1]{0:T(128)} %bitcast.2.plane_ref, s32[1]{0:T(128)} %bitcast.3.own_ref, s32[128]{0:T(128)} %order_ref.3, bf16[512,128]{1,0:T(8,128)(2,1)} %q_ref.1, bf16[512,128]{1,0:T(8,128)(2,1)} %k_ref.1, ...), custom_call_target="tpu_custom_call" | custom-call | tf_op jit(solution)/shard_map/pack/pallas_call | solution.py:195
  1.9 11.2 %collective-permute-start.1 = (bf16[512,128]{1,0:T(8,128)(2,1)S(1)}, bf16[512,128]{1,0:T(8,128)(2,1)S(1)}, u32[]{:S(2)}, u32[]{:S(2)}) collective-permute-start(bf16[512,128]{1,0:T(8,128)(2,1)S(1)} %get-tuple-element.8.kv0), channel_id=1, source_target_pairs={{0,64},{2,66},{4,68},{6,70},{8,72},{10,74},{12,76},{14,78},{16,80}... | collective-permute-start | bytes 393224 | tf_op jit(solution)/shard_map/ppermute | solution.py:48
  13.1 2.2 %collective-permute-start = (bf16[512,128]{1,0:T(8,128)(2,1)S(1)}, bf16[512,128]{1,0:T(8,128)(2,1)S(1)}, u32[]{:S(2)}, u32[]{:S(2)}) collective-permute-start(bf16[512,128]{1,0:T(8,128)(2,1)S(1)} %get-tuple-element.8.kv0), channel_id=1, source_target_pairs={{0,32},{2,34},{4,36},{6,38},{8,40},{10,42},{12,44},{14,46},{16,48}... | collective-permute-start | bytes 393224 | tf_op jit(solution)/shard_map/ppermute | solution.py:48
  15.3 4.4 %all-to-all-start = ((bf16[8,256,128]{2,1,0:T(8,128)(2,1)}), bf16[8,256,128]{2,1,0:T(8,128)(2,1)S(1)}, u32[]{:S(2)}, u32[]{:S(2)}) async-start(bf16[8,256,128]{2,1,0:T(8,128)(2,1)} %get-tuple-element.7), calls=%async_computation | async-start | bytes 1048576 | tf_op jit(solution)/shard_map/all_to_all | solution.py:206
  19.7 0.0 collective-permute-done.1.kv2
  19.7 0.0 collective-permute-done.kv1
  19.8 5.7 %collective-permute-start.2 = (bf16[1024,128]{1,0:T(8,128)(2,1)S(1)}, bf16[1024,128]{1,0:T(8,128)(2,1)S(1)}, u32[]{:S(2)}, u32[]{:S(2)}) collective-permute-start(bf16[1024,128]{1,0:T(8,128)(2,1)S(1)} %pad_maximum_fusion), channel_id=1, source_target_pairs={{0,64},{2,66},{4,68},{6,70},{8,72},{10,74},{12,76},{14,78},{16,80}... | collective-permute-start | bytes 786440 | tf_op jit(solution)/shard_map/ppermute | solution.py:48
  25.5 1.3 %limits.1.d_ref = s32[4,256,128]{2,1,0:T(8,128)S(1)} custom-call(s32[1]{0:T(128)} %bitcast.ctx_ref, s32[1]{0:T(128)} %bitcast.1.core_ref, s32[1]{0:T(128)} %bitcast.2.plane_ref, s32[1]{0:T(128)} %bitcast.3.own_ref, s32[16]{0:T(128)} %length_ref.1), custom_call_target="tpu_custom_call" | custom-call | flops 4000000 | bytes 600000 | tf_op jit(solution)/shard_map/limits/pallas_call | solution.py:208
  26.8 3.8 %collective-permute-done.2.kv34 = bf16[1024,128]{1,0:T(8,128)(2,1)S(1)} collective-permute-done((bf16[1024,128]{1,0:T(8,128)(2,1)S(1)}, bf16[1024,128]{1,0:T(8,128)(2,1)S(1)}, u32[]{:S(2)}, u32[]{:S(2)}) %collective-permute-start.2) | collective-permute-done | bytes 262176 | tf_op jit(solution)/shard_map/ppermute | solution.py:48
  30.6 0.0 all-to-all-done.q_ref
  30.6 3.9 %attend.1 = bf16[8,272,128]{2,1,0:T(8,128)(2,1)S(1)} custom-call(s32[1]{0:T(128)} %bitcast.ctx_ref, s32[1]{0:T(128)} %bitcast.1.core_ref, s32[1]{0:T(128)} %bitcast.2.plane_ref, s32[1]{0:T(128)} %bitcast.3.own_ref, bf16[8,256,128]{2,1,0:T(8,128)(2,1)S(1)} %all-to-all-done.q_ref, s32[4,256,128]{2,1,0:T(8,128)S(1)} %limits.1.d_ref, ...), custom_call_target="tpu_custom_call" | custom-call | tf_op jit(solution)/shard_map/attend/pallas_call | solution.py:217
  34.5 21.1 %all_to_all.10.r_ref = bf16[8,272,128]{2,1,0:T(8,128)(2,1)S(1)} all-to-all(bf16[8,272,128]{2,1,0:T(8,128)(2,1)S(1)} %attend.1), channel_id=1, replica_groups=mesh['y_hi'=2,'z'=8,'x'=4,'y_lo'=4,'core'=2] {'x','core'}, dimensions={0} | all-to-all | bytes 1114112 | tf_op jit(solution)/shard_map/all_to_all | solution.py:229
  55.6 1.8 %merge.1 = bf16[512,128]{1,0:T(8,128)(2,1)} custom-call(s32[1]{0:T(128)} %bitcast.ctx_ref, s32[1]{0:T(128)} %bitcast.1.core_ref, s32[1]{0:T(128)} %bitcast.2.plane_ref, s32[1]{0:T(128)} %bitcast.3.own_ref, s32[128]{0:T(128)} %order_ref.3, bf16[8,272,128]{2,1,0:T(8,128)(2,1)S(1)} %all_to_all.10.r_ref), custom_call_target="tpu_custom_call" | custom-call | tf_op jit(solution)/shard_map/merge/pallas_call | solution.py:231
  (1 shorter events, 0.0 us)
Async XLA Ops:
  1.9 17.8 %collective-permute-start.1 = (bf16[512,128]{1,0:T(8,128)(2,1)S(1)}, bf16[512,128]{1,0:T(8,128)(2,1)S(1)}, u32[]{:S(2)}, u32[]{:S(2)}) collective-permute-start(bf16[512,128]{1,0:T(8,128)(2,1)S(1)} %get-tuple-element.8.kv0), channel_id=1, source_target_pairs={{0,64},{2,66},{4,68},{6,70},{8,72},{10,74},{12,76},{14,78},{16,80}... | collective-permute-start | bytes 393224 | tf_op jit(solution)/shard_map/ppermute | solution.py:48
  13.1 6.6 %collective-permute-start = (bf16[512,128]{1,0:T(8,128)(2,1)S(1)}, bf16[512,128]{1,0:T(8,128)(2,1)S(1)}, u32[]{:S(2)}, u32[]{:S(2)}) collective-permute-start(bf16[512,128]{1,0:T(8,128)(2,1)S(1)} %get-tuple-element.8.kv0), channel_id=1, source_target_pairs={{0,32},{2,34},{4,36},{6,38},{8,40},{10,42},{12,44},{14,46},{16,48}... | collective-permute-start | bytes 393224 | tf_op jit(solution)/shard_map/ppermute | solution.py:48
  15.3 15.3 %all-to-all-start = ((bf16[8,256,128]{2,1,0:T(8,128)(2,1)}), bf16[8,256,128]{2,1,0:T(8,128)(2,1)S(1)}, u32[]{:S(2)}, u32[]{:S(2)}) async-start(bf16[8,256,128]{2,1,0:T(8,128)(2,1)} %get-tuple-element.7), calls=%async_computation | async-start | bytes 1048576 | tf_op jit(solution)/shard_map/all_to_all | solution.py:206
  19.8 10.8 %collective-permute-start.2 = (bf16[1024,128]{1,0:T(8,128)(2,1)S(1)}, bf16[1024,128]{1,0:T(8,128)(2,1)S(1)}, u32[]{:S(2)}, u32[]{:S(2)}) collective-permute-start(bf16[1024,128]{1,0:T(8,128)(2,1)S(1)} %pad_maximum_fusion), channel_id=1, source_target_pairs={{0,64},{2,66},{4,68},{6,70},{8,72},{10,74},{12,76},{14,78},{16,80}... | collective-permute-start | bytes 786440 | tf_op jit(solution)/shard_map/ppermute | solution.py:48

commit v2 on v1

--- a/solution.py
+++ b/solution.py
@@ -8,6 +8,7 @@
 from jax.experimental.pallas import tpu as pltpu
 from jax.sharding import Mesh
 from jax.sharding import PartitionSpec as P
+
 
 DH = 128
 CH = 256
@@ -38,7 +39,7 @@
                     folded = target >= PLANES
                     other = 2 * PLANES - 1 - target if folded else target
                     column = 3 - x if folded and core == 0 else x
-                    row = y_lo if plane // 8 == other // 8 else 3 - y_lo
+                    row = y_lo if plane // 8 == other // 8 else (y_lo ^ 2 if shift == 1 else 3 - y_lo)
                     source = device(plane // 8, plane % 8, x, y_lo, core)
                     pairs.append((source, device(other // 8, other % 8, column, row, int(folded))))
     return pairs
@@ -52,17 +53,16 @@
     return jnp.where(order_ref[2 * ctx_ref[0]] == ctx_ref[0], 0, 1)
 
 
-def pack_kernel(ctx_ref, core_ref, plane_ref, own_ref, order_ref, q_ref, k_ref, v_ref, qs_ref, kv_ref):
+def pack_kernel(
+    ctx_ref, core_ref, plane_ref, own_ref, order_ref, q_ref, k_ref, v_ref, q_out, kv_out
+):
     low = lower_slot(order_ref, ctx_ref)
     own = jnp.where(core_ref[0] == 0, low, 1 - low)
     start = pl.multiple_of(own * CH, CH)
-    kv_ref[:CH, :] = k_ref[pl.ds(start, CH), :]
-    kv_ref[CH:, :] = v_ref[pl.ds(start, CH), :]
-    for flow in range(2):
-        slot = pl.multiple_of((low if flow == 0 else 1 - low) * CH, CH)
-        block = q_ref[pl.ds(slot, CH), :]
-        for x in range(4):
-            qs_ref[2 * x + flow] = block
+    kv_out[:CH, :] = k_ref[pl.ds(start, CH), :]
+    kv_out[CH:, :] = v_ref[pl.ds(start, CH), :]
+    q_out[0] = q_ref[pl.ds(pl.multiple_of(low * CH, CH), CH), :]
+    q_out[1] = q_ref[pl.ds(pl.multiple_of((1 - low) * CH, CH), CH), :]
 
 
 def limits_kernel(ctx_ref, core_ref, plane_ref, own_ref, length_ref, d_ref):
@@ -78,51 +78,94 @@
         d_ref[column] = lanes - start
 
 
-def attend_kernel(ctx_ref, core_ref, plane_ref, own_ref, q_ref, d_ref, kv0, kv1, kv2, kv34, o_ref, k_all, v_all):
-    for slot, ref in enumerate((kv0, kv1, kv2, kv34.at[: 2 * CH], kv34.at[2 * CH :])):
+def load_keys(refs, k_all, v_all):
+    for slot, ref in enumerate(refs):
         k_all[slot] = ref[:CH, :]
         v_all[slot, :, :DH] = ref[CH:, :]
         v_all[slot, :, DH:] = jnp.ones((CH, DH), jnp.bfloat16)
+
+
+def weigh(q, pieces, top, total):
+    scores = []
+    best = None
+    for key, _, mask in pieces:
+        score = lax.dot_general(
+            q, key, (((1,), (1,)), ((), ())), preferred_element_type=jnp.float32
+        )
+        score = jnp.where(mask, score, NEGATIVE)
+        scores.append(score)
+        best = score if best is None else jnp.maximum(best, score)
+    best = jnp.maximum(jnp.max(best, axis=1, keepdims=True), FLOOR) * COEF
+    if top is not None:
+        best = jnp.maximum(best, top)
+        factor = jnp.exp2(top - best)
+        total = total * jnp.concatenate([factor, factor], axis=1)
+        wide = jnp.concatenate([best, best], axis=1)
+    else:
+        wide = best
+    for (_, value, _), score in zip(pieces, scores):
+        weight = jnp.exp2(score * COEF - wide).astype(jnp.bfloat16)
+        term = jnp.dot(weight, value, preferred_element_type=jnp.float32)
+        total = term if total is None else total + term
+    return best, total
+
+
+def bounds(d_ref, column):
+    half = d_ref[column]
+    return jnp.concatenate([half, half + DH], axis=1)
+
+
+def begin_kernel(
+    ctx_ref, core_ref, plane_ref, own_ref, q_ref, d_ref, kv0, kv1, kv2, top_ref, sum_ref, k_all, v_all
+):
+    load_keys((kv0, kv1, kv2), k_all, v_all)
     core, plane, own = core_ref[0], plane_ref[0], own_ref[0]
     causal = lax.broadcasted_iota(jnp.int32, (CH, CH), 0) >= lax.broadcasted_iota(
         jnp.int32, (CH, CH), 1
     )
+    for turn in range(4):
+        column = lax.rem(own + turn, 4)
+        x = jnp.where(core == 0, column, 3 - column)
+        d = bounds(d_ref, column)
+        masks = [(slot, d >= -CH * (4 * (plane - slot) + own)) for slot in range(3)]
+        if turn == 0:
+            masks[0] = (0, masks[0][1] & causal)
+        else:
+            masks = masks[1:]
+        for head in range(2):
+            block = 2 * x + head
+            pieces = [(k_all[slot], v_all[slot], mask) for slot, mask in masks]
+            best, total = weigh(q_ref[block], pieces, None, None)
+            top_ref[block] = jnp.broadcast_to(best, (CH, DH))
+            sum_ref[block] = total
+
+
+def finish_kernel(
+    ctx_ref, core_ref, plane_ref, own_ref, q_ref, d_ref, kv0, pair, top_ref, sum_ref, o_ref, k_all, v_all
+):
+    load_keys((kv0, pair.at[: 2 * CH], pair.at[2 * CH :]), k_all, v_all)
+    core, plane, own = core_ref[0], plane_ref[0], own_ref[0]
     eye = lax.broadcasted_iota(jnp.int32, (DH, DH), 0) == lax.broadcasted_iota(
         jnp.int32, (DH, DH), 1
     )
     extra_row = lax.broadcasted_iota(jnp.int32, (EXTRA, DH), 0)
-
-    def one(turn, column, slots):
+    for turn in range(4):
+        column = lax.rem(own + turn, 4)
         x = jnp.where(core == 0, column, 3 - column)
-        half = d_ref[column]
-        d = jnp.concatenate([half, half + DH], axis=1)
-        masks = []
-        for slot in slots:
-            mask = d >= -CH * (4 * (plane - slot) + own)
-            if turn == 0 and isinstance(slot, int) and slot == 0:
-                mask = mask & causal
-            masks.append(mask)
+        d = bounds(d_ref, column)
+        edge = jnp.where(column > own, 0, 2)
+        age = jnp.where(column > own, 0, 4)
+        masks = [
+            (1, d >= -CH * (4 * (plane - 3) + own)),
+            (edge, d >= -CH * (4 * (plane - age) + own)),
+        ]
         for head in range(2):
             block = 2 * x + head
-            q = q_ref[block]
-            scores = []
-            top = None
-            for slot, mask in zip(slots, masks):
-                score = lax.dot_general(
-                    q, k_all[slot], (((1,), (1,)), ((), ())), preferred_element_type=jnp.float32
-                )
-                score = jnp.where(mask, score, NEGATIVE)
-                scores.append(score)
-                top = score if top is None else jnp.maximum(top, score)
-            top = jnp.maximum(jnp.max(top, axis=1, keepdims=True), FLOOR) * COEF
-            total = None
-            for slot, score in zip(slots, scores):
-                weight = jnp.exp2(score * COEF - top).astype(jnp.bfloat16)
-                term = jnp.dot(weight, v_all[slot], preferred_element_type=jnp.float32)
-                total = term if total is None else total + term
-            mass = total[:, DH:]
-            o_ref[block, :CH, :] = (total[:, :DH] / jnp.maximum(mass, 1e-30)).astype(jnp.bfloat16)
-            level = top + jnp.log2(jnp.maximum(mass, 1e-30))
+            pieces = [(k_all[slot], v_all[slot], mask) for slot, mask in masks]
+            top, total = weigh(q_ref[block], pieces, top_ref[block], sum_ref[block])
+            mass = jnp.maximum(total[:, DH:], 1e-30)
+            o_ref[block, :CH, :] = (total[:, :DH] / mass).astype(jnp.bfloat16)
+            level = top + jnp.log2(mass)
             extra = jnp.zeros((EXTRA, DH), jnp.float32)
             for group in range(2):
                 line = jnp.sum(
@@ -133,11 +176,6 @@
                     extra = jnp.where(extra_row == 2 * piece + group, rounded, extra)
                     line = line - rounded
             o_ref[block, CH:, :] = extra.astype(jnp.bfloat16)
-
-    one(0, own, (0, 1, 2, 3, 4))
-    for turn in range(1, 4):
-        column = lax.rem(own + turn, 4)
-        one(turn, column, (jnp.where(column > own, 0, 4), 1, 2, 3))
 
 
 def merge_kernel(ctx_ref, core_ref, plane_ref, own_ref, order_ref, r_ref, out_ref, w_ref):
@@ -192,9 +230,9 @@
     column = jnp.where(first, ctx % 4, 3 - ctx % 4)
     meta = tuple(part.reshape(1) for part in (ctx, core, z_line, column))
 
-    sent, own = pl.pallas_call(
+    both, own = pl.pallas_call(
         pack_kernel,
-        out_shape=(pltpu.VMEM((8, CH, DH), jnp.bfloat16), pltpu.VMEM((2 * CH, DH), jnp.bfloat16)),
+        out_shape=(pltpu.VMEM((2, CH, DH), jnp.bfloat16), pltpu.VMEM((2 * CH, DH), jnp.bfloat16)),
         in_specs=in_smem(5) + in_vmem(3),
         out_specs=tuple(in_vmem(2)),
         name="pack",
@@ -202,8 +240,9 @@
 
     near = shifted(own, 1)
     two = shifted(own, 2)
+    sent = jnp.broadcast_to(both[None], (4, 2, CH, DH)).reshape(8, CH, DH)
+    asked = lax.all_to_all(sent, ("x", "core"), 0, 0, tiled=True)
     pair = shifted(jnp.concatenate([near, two]), 2)
-    asked = lax.all_to_all(sent, ("x", "core"), 0, 0, tiled=True)
 
     limits = pl.pallas_call(
         limits_kernel,
@@ -212,19 +251,35 @@
         out_specs=in_vmem(1)[0],
         cost_estimate=pl.CostEstimate(flops=4000000, bytes_accessed=600000, transcendentals=0),
         name="limits",
+            compiler_params=pltpu.CompilerParams(vmem_limit_bytes=24 << 20),
     )(*meta, doc_lengths)
 
+    def keys_scratch():
+        return [
+            pltpu.VMEM((3, CH, DH), jnp.bfloat16),
+            pltpu.VMEM((3, CH, 2 * DH), jnp.bfloat16),
+        ]
+
+    tops, sums = pl.pallas_call(
+        begin_kernel,
+        out_shape=(pltpu.VMEM((8, CH, DH), jnp.float32), pltpu.VMEM((8, CH, 2 * DH), jnp.float32)),
+        in_specs=in_smem(4) + in_vmem(5),
+        out_specs=tuple(in_vmem(2)),
+        scratch_shapes=keys_scratch(),
+        cost_estimate=pl.CostEstimate(flops=1000000000, bytes_accessed=1000000, transcendentals=1200000),
+        name="begin",
+        compiler_params=pltpu.CompilerParams(vmem_limit_bytes=24 << 20),
+    )(*meta, *map(close, (asked, limits, own, near, two)))
+
     partial = pl.pallas_call(
-        attend_kernel,
+        finish_kernel,
         out_shape=pltpu.VMEM((8, CH + EXTRA, DH), jnp.bfloat16),
         in_specs=in_smem(4) + in_vmem(6),
         out_specs=in_vmem(1)[0],
-        scratch_shapes=[
-            pltpu.VMEM((5, CH, DH), jnp.bfloat16),
-            pltpu.VMEM((5, CH, 2 * DH), jnp.bfloat16),
-        ],
-        name="attend",
-    )(*meta, *map(close, (asked, limits, own, near, two, pair)))
+        scratch_shapes=keys_scratch(),
+        name="finish",
+            compiler_params=pltpu.CompilerParams(vmem_limit_bytes=24 << 20),
+    )(*meta, *map(close, (asked, limits, own, pair, tops, sums)))
 
     back = lax.all_to_all(partial, ("x", "core"), 0, 0, tiled=True)
 
@@ -241,6 +296,4 @@
 def solution(mesh):
     parts = Mesh(mesh.devices.reshape(SIZES), AXES)
     placed = (P(CTX, HEAD), P(CTX, None), P(CTX, None), P(), P())
-    return jax.shard_map(
-        body, mesh=parts, in_specs=placed, out_specs=P(CTX, HEAD), check_vma=False
-    )
+    return jax.shard_map(body, mesh=parts, in_specs=placed, out_specs=P(CTX, HEAD), check_vma=False)

time: 57.7 us -> 59.6 us (1.033)
  starting transfers between devices: 23.5 us -> 24.8 us
  local copies, waits for them, and re-layouts: 0 us -> 0.86 us
    broadcast_in_dim x0 -> x1, local copies, waits for them, and re-layouts: none -> 0.86 us  [body(): sent = jnp.broadcast_to(both[None], (4, 2, CH, DH)).reshape(8, CH, DH)]
    ppermute x3, starting transfers between devices: 19.1 us -> 19.8 us  [shifted(): return lax.ppermute(block, AXES, plane_pairs(shift))]
    pallas_call x2 -> x3, Pallas kernels: 5.79 us -> 5.37 us  [the longest x1 2.16 us: body(): pl.pallas_call(finish_kernel, out_shape=pltpu.VMEM((8, CH + EXTRA, DH), j...]
  transfers between devices with their start and end apart: 4 -> 4, of which waited for: 1 -> 1; matrix products, arithmetic and copies ran while one was open for 0% -> 0% of each run, Pallas kernels for 2% -> 6%
where the time goes in v2:
time: 59.6 us; the launch traced here: 59.3 us
  starting transfers between devices  24.8 us (42%)
  blocking collectives  21.5 us (36%)
  Pallas kernels  8.34 us (14%)
  waiting for transfers between devices  3.74 us (6%)
  local copies, waits for them, and re-layouts  0.86 us (1%)
    all_to_all x1, blocking collectives, body(): back = lax.all_to_all(partial, ('x', 'core'), 0, 0, tiled=True)  21.5 us
    ppermute x3, starting transfers between devices, shifted(): return lax.ppermute(block, AXES, plane_pairs(shift))  19.8 us
    all_to_all x1, starting transfers between devices, body(): asked = lax.all_to_all(sent, ('x', 'core'), 0, 0, tiled=True)  4.97 us
    ppermute x3, waiting for transfers between devices, shifted(): return lax.ppermute(block, AXES, plane_pairs(shift))  3.74 us
    pallas_call x1, Pallas kernels, body(): pl.pallas_call(finish_kernel, out_shape=pltpu.VMEM((8, CH + EXTRA, DH), j...  2.16 us
    pallas_call x1, Pallas kernels, body(): pl.pallas_call(begin_kernel, out_shape=(pltpu.VMEM((8, CH, DH), jnp.float...  2.13 us
    pallas_call x1, Pallas kernels, body(): pl.pallas_call(merge_kernel, out_shape=struct((2 * CH, DH)), in_specs=in_...  1.84 us
  transfers between devices with their start and end apart: 4, of which 1 were waited for; matrix products, arithmetic and copies ran while one was open for 0% of the time, Pallas kernels for 6%

profile of v2, /device:TPU:41, one launch (start us, length us, event | category | flops | bytes accessed | tf_op | source)
XLA Modules:
  0.0 59.3 jit_solution(5602977441968678452)
XLA Ops:
  0.0 0.0 copy-start
  0.0 1.1 %pack.1 = (bf16[2,256,128]{2,1,0:T(8,128)(2,1)S(1)}, bf16[512,128]{1,0:T(8,128)(2,1)S(1)}) custom-call(s32[1]{0:T(128)} %bitcast.ctx_ref, s32[1]{0:T(128)} %bitcast.1.core_ref, s32[1]{0:T(128)} %bitcast.2.plane_ref, s32[1]{0:T(128)} %bitcast.3.own_ref, s32[128]{0:T(128)} %order_ref.3, bf16[512,128]{1,0:T(8,128)(2,1)} %q_ref.1, bf16[512,128]{1,0:T(8,128)(2,1)} %k_ref.1, ...), custom_call_target="tpu_custom_call" | custom-call | tf_op jit(solution)/shard_map/pack/pallas_call | solution.py:233
  1.1 0.9 %broadcast_in_dim.2 = bf16[4,2,256,128]{3,2,1,0:T(8,128)(2,1)} broadcast(bf16[2,256,128]{2,1,0:T(8,128)(2,1)S(1)} %get-tuple-element.9), dimensions={1,2,3} | broadcast | bytes 655360 | tf_op jit(solution)/shard_map/broadcast_in_dim | solution.py:243
  1.9 5.0 %all-to-all-start = ((bf16[8,256,128]{2,1,0:T(8,128)(2,1)}), bf16[8,256,128]{2,1,0:T(8,128)(2,1)S(1)}, u32[]{:S(2)}, u32[]{:S(2)}) async-start(bf16[8,256,128]{2,1,0:T(8,128)(2,1)} %bitcast.4), calls=%async_computation | async-start | bytes 1048576 | tf_op jit(solution)/shard_map/all_to_all | solution.py:244
  6.9 11.2 %collective-permute-start.1 = (bf16[512,128]{1,0:T(8,128)(2,1)S(1)}, bf16[512,128]{1,0:T(8,128)(2,1)S(1)}, u32[]{:S(2)}, u32[]{:S(2)}) collective-permute-start(bf16[512,128]{1,0:T(8,128)(2,1)S(1)} %get-tuple-element.10.kv0), channel_id=1, source_target_pairs={{0,64},{2,66},{4,68},{6,70},{8,72},{10,74},{12,76},{14,78},{16,80}... | collective-permute-start | bytes 393224 | tf_op jit(solution)/shard_map/ppermute | solution.py:49
  18.1 2.3 %collective-permute-start = (bf16[512,128]{1,0:T(8,128)(2,1)S(1)}, bf16[512,128]{1,0:T(8,128)(2,1)S(1)}, u32[]{:S(2)}, u32[]{:S(2)}) collective-permute-start(bf16[512,128]{1,0:T(8,128)(2,1)S(1)} %get-tuple-element.10.kv0), channel_id=1, source_target_pairs={{0,32},{2,34},{4,36},{6,38},{8,40},{10,42},{12,44},{14,46},{16,48}... | collective-permute-start | bytes 393224 | tf_op jit(solution)/shard_map/ppermute | solution.py:49
  20.4 0.0 collective-permute-done.1.kv2
  20.4 3.7 %collective-permute-done.kv1 = bf16[512,128]{1,0:T(8,128)(2,1)S(1)} collective-permute-done((bf16[512,128]{1,0:T(8,128)(2,1)S(1)}, bf16[512,128]{1,0:T(8,128)(2,1)S(1)}, u32[]{:S(2)}, u32[]{:S(2)}) %collective-permute-start) | collective-permute-done | bytes 131104 | tf_op jit(solution)/shard_map/ppermute | solution.py:49
  24.2 6.3 %collective-permute-start.2 = (bf16[1024,128]{1,0:T(8,128)(2,1)S(1)}, bf16[1024,128]{1,0:T(8,128)(2,1)S(1)}, u32[]{:S(2)}, u32[]{:S(2)}) collective-permute-start(bf16[1024,128]{1,0:T(8,128)(2,1)S(1)} %pad_maximum_fusion), channel_id=1, source_target_pairs={{0,64},{2,66},{4,68},{6,70},{8,72},{10,74},{12,76},{14,78},{16,80}... | collective-permute-start | bytes 786440 | tf_op jit(solution)/shard_map/ppermute | solution.py:49
  30.5 0.0 copy-done
  30.5 1.1 %limits.1.d_ref = s32[4,256,128]{2,1,0:T(8,128)S(1)} custom-call(s32[1]{0:T(128)} %bitcast.ctx_ref, s32[1]{0:T(128)} %bitcast.1.core_ref, s32[1]{0:T(128)} %bitcast.2.plane_ref, s32[1]{0:T(128)} %bitcast.3.own_ref, s32[16]{0:T(128)S(1)} %copy-done), custom_call_target="tpu_custom_call" | custom-call | flops 4000000 | bytes 600000 | tf_op jit(solution)/shard_map/limits/pallas_call | solution.py:247
  31.7 0.0 all-to-all-done.q_ref
  31.7 2.1 %begin.1 = (f32[8,256,128]{2,1,0:T(8,128)S(1)}, f32[8,256,256]{2,1,0:T(8,128)S(1)}) custom-call(s32[1]{0:T(128)} %bitcast.ctx_ref, s32[1]{0:T(128)} %bitcast.1.core_ref, s32[1]{0:T(128)} %bitcast.2.plane_ref, s32[1]{0:T(128)} %bitcast.3.own_ref, bf16[8,256,128]{2,1,0:T(8,128)(2,1)S(1)} %all-to-all-done.q_ref, s32[4,256,128]{2,1,0:T(8,128)S(1)} %limits.1.d_ref, ...), custom_call_target="tpu_custom_call" | custom-call | flops 1000000000 | bytes 1000000 | tf_op jit(solution)/shard_map/begin/pallas_call | solution.py:263
  33.8 0.0 collective-permute-done.2.pair
  33.8 2.2 %finish.1 = bf16[8,272,128]{2,1,0:T(8,128)(2,1)S(1)} custom-call(s32[1]{0:T(128)} %bitcast.ctx_ref, s32[1]{0:T(128)} %bitcast.1.core_ref, s32[1]{0:T(128)} %bitcast.2.plane_ref, s32[1]{0:T(128)} %bitcast.3.own_ref, bf16[8,256,128]{2,1,0:T(8,128)(2,1)S(1)} %all-to-all-done.q_ref, s32[4,256,128]{2,1,0:T(8,128)S(1)} %limits.1.d_ref, ...), custom_call_target="tpu_custom_call" | custom-call | tf_op jit(solution)/shard_map/finish/pallas_call | solution.py:274
  36.0 21.5 %all_to_all.10.r_ref = bf16[8,272,128]{2,1,0:T(8,128)(2,1)S(1)} all-to-all(bf16[8,272,128]{2,1,0:T(8,128)(2,1)S(1)} %finish.1), channel_id=1, replica_groups=mesh['y_hi'=2,'z'=8,'x'=4,'y_lo'=4,'core'=2] {'x','core'}, dimensions={0} | all-to-all | bytes 1114112 | tf_op jit(solution)/shard_map/all_to_all | solution.py:284
  57.5 1.8 %merge.1 = bf16[512,128]{1,0:T(8,128)(2,1)} custom-call(s32[1]{0:T(128)} %bitcast.ctx_ref, s32[1]{0:T(128)} %bitcast.1.core_ref, s32[1]{0:T(128)} %bitcast.2.plane_ref, s32[1]{0:T(128)} %bitcast.3.own_ref, s32[128]{0:T(128)} %order_ref.3, bf16[8,272,128]{2,1,0:T(8,128)(2,1)S(1)} %all_to_all.10.r_ref), custom_call_target="tpu_custom_call" | custom-call | tf_op jit(solution)/shard_map/merge/pallas_call | solution.py:286
  (1 shorter events, 0.0 us)
Async XLA Ops:
  0.0 30.5 %copy-start = (s32[16]{0:T(128)S(1)}, s32[16]{0:T(128)}, u32[]{:S(2)}) copy-start(s32[16]{0:T(128)} %length_ref.1) | copy-start | bytes 196
  1.9 29.7 %all-to-all-start = ((bf16[8,256,128]{2,1,0:T(8,128)(2,1)}), bf16[8,256,128]{2,1,0:T(8,128)(2,1)S(1)}, u32[]{:S(2)}, u32[]{:S(2)}) async-start(bf16[8,256,128]{2,1,0:T(8,128)(2,1)} %bitcast.4), calls=%async_computation | async-start | bytes 1048576 | tf_op jit(solution)/shard_map/all_to_all | solution.py:244
  6.9 13.5 %collective-permute-start.1 = (bf16[512,128]{1,0:T(8,128)(2,1)S(1)}, bf16[512,128]{1,0:T(8,128)(2,1)S(1)}, u32[]{:S(2)}, u32[]{:S(2)}) collective-permute-start(bf16[512,128]{1,0:T(8,128)(2,1)S(1)} %get-tuple-element.10.kv0), channel_id=1, source_target_pairs={{0,64},{2,66},{4,68},{6,70},{8,72},{10,74},{12,76},{14,78},{16,80}... | collective-permute-start | bytes 393224 | tf_op jit(solution)/shard_map/ppermute | solution.py:49
  18.1 6.0 %collective-permute-start = (bf16[512,128]{1,0:T(8,128)(2,1)S(1)}, bf16[512,128]{1,0:T(8,128)(2,1)S(1)}, u32[]{:S(2)}, u32[]{:S(2)}) collective-permute-start(bf16[512,128]{1,0:T(8,128)(2,1)S(1)} %get-tuple-element.10.kv0), channel_id=1, source_target_pairs={{0,32},{2,34},{4,36},{6,38},{8,40},{10,42},{12,44},{14,46},{16,48}... | collective-permute-start | bytes 393224 | tf_op jit(solution)/shard_map/ppermute | solution.py:49
  24.2 9.7 %collective-permute-start.2 = (bf16[1024,128]{1,0:T(8,128)(2,1)S(1)}, bf16[1024,128]{1,0:T(8,128)(2,1)S(1)}, u32[]{:S(2)}, u32[]{:S(2)}) collective-permute-start(bf16[1024,128]{1,0:T(8,128)(2,1)S(1)} %pad_maximum_fusion), channel_id=1, source_target_pairs={{0,64},{2,66},{4,68},{6,70},{8,72},{10,74},{12,76},{14,78},{16,80}... | collective-permute-start | bytes 786440 | tf_op jit(solution)/shard_map/ppermute | solution.py:49
